TPU v7x, 32 devices: a whole 2x2x4 slice. The times are simulated.
32 devices in a mesh: replica: 2 (over core), shard: 16 (over z, y, x).
Axes of the slice: x: 2, y: 2, z: 4, core: 2. Of those that a mesh axis runs over, the one named last changes fastest.
Arguments:
- inner_params: bfloat16 [2, 15360, 4096], P('replica', 'shard'), may hold values from -6 to 6
- anchor: float32 [15360, 4096], P('shard'), may hold values from -6 to 6
- momentum: float32 [15360, 4096], P('shard'), may hold values from -2 to 2
- first_moment: bfloat16 [2, 15360, 4096], P('replica', 'shard'), may hold values from -0.59765625 to 0.59765625
- second_moment: bfloat16 [2, 15360, 4096], P('replica', 'shard'), may hold values from 0.0009994507 to 0.099609375
- activations: bfloat16 [2, 64, 4096], P('replica', 'shard'), may hold values from -6 to 6
- cotangent: bfloat16 [2, 15360, 64], P('replica', 'shard'), may hold values from -6 to 6
- spare_index: int32 [16], P('shard'), may hold values from 0 to 1
- peer_index: int32 [16], P('shard'), may hold values from 0 to 1
Outputs:
- anchor_new: float32 [15360, 4096], P('shard')
- momentum_new: float32 [15360, 4096], P('shard')
- update: float32 [2, 15360, 4096], P('replica', 'shard')
Inputs may be any that keep to these rules, and one draw needn't show every extreme that they name: `spare_index`: a replica index for each block. `peer_index`: a replica index for each block; where it equals spare_index the spare keeps its own moments.
All inputs are finite; a program needn't handle non-finite values.
Results may differ from a plain program's by a relative error of at most 0.0018.
Values may be sent and summed in bfloat16 or wider, within the bound.
No kernel may reach another device: no remote copies, remote signals or barrier semaphores. Data moves between devices by JAX's collectives and lax.ppermute only.
A program may use at most 192 MiB of HBM per device.

v0:
```python
import math

import jax
import jax.numpy as jnp
from jax import lax
from jax.sharding import PartitionSpec as P

outer_rate = 0.7
nesterov_mu = 0.9
beta_one = 0.9
beta_two = 0.95
bias_one = 1.0 - 0.9**40
bias_two = 1.0 - 0.95**40
adam_eps = 1e-08
decay_rate = 0.1


def from_root(block, axis, holder):
    block = jnp.where(lax.axis_index(axis) == holder, block, jnp.zeros_like(block))
    return lax.psum(block, axis)


def slope(pre):
    sigma = jax.nn.sigmoid(pre)
    return sigma * (1.0 + pre * (1.0 - sigma))


def local(
    inner_params,
    anchor,
    momentum,
    first_moment,
    second_moment,
    activations,
    cotangent,
    spare_index,
    peer_index,
):
    replicas = lax.axis_size("replica")
    position = lax.axis_index("replica")
    spare_slot = spare_index[0]
    peer_slot = peer_index[0]
    healthy = (position != spare_slot).astype(jnp.float32)
    difference = (anchor - inner_params[0].astype(jnp.float32)) * healthy
    summed = lax.psum(difference, "replica")
    average = summed / (replicas - 1)
    momentum_new = nesterov_mu * momentum + average
    anchor_new = anchor - outer_rate * (average + nesterov_mu * momentum_new)
    received = (
        from_root(first_moment, "replica", peer_slot),
        from_root(second_moment, "replica", peer_slot),
    )
    is_spare = position == spare_slot
    first_used = jnp.where(is_spare, received[0], first_moment)[0].astype(jnp.float32)
    second_used = jnp.where(is_spare, received[1], second_moment)[0].astype(jnp.float32)
    weights = anchor_new.astype(jnp.bfloat16)
    root = math.sqrt(weights.shape[1])
    cot_local = cotangent[0]
    tokens_part = lax.all_gather(activations, "shard", axis=1, tiled=True)[0]
    pre = (
        lax.dot_general(
            weights, tokens_part, (((1,), (1,)), ((), ())), preferred_element_type=jnp.float32
        )
        / root
    )
    grad_pre = (cot_local.astype(jnp.float32) * slope(pre)).astype(jnp.bfloat16)
    gradient = jnp.dot(grad_pre, tokens_part, preferred_element_type=jnp.float32) / root
    first = beta_one * first_used + (1.0 - beta_one) * gradient
    second = beta_two * second_used + (1.0 - beta_two) * gradient * gradient
    update = first / bias_one / (jnp.sqrt(second / bias_two) + adam_eps) + decay_rate * anchor_new
    return (anchor_new, momentum_new, update[None])


def solution(mesh):
    placed = (
        P("replica", "shard", None),
        P("shard", None),
        P("shard", None),
        P("replica", "shard", None),
        P("replica", "shard", None),
        P("replica", "shard", None),
        P("replica", "shard", None),
        P("shard"),
        P("shard"),
    )
    return jax.shard_map(
        local,
        mesh=mesh,
        in_specs=placed,
        out_specs=(P("shard", None), P("shard", None), P("replica", "shard", None)),
        check_vma=False,
    )
```

profile of v0, /device:TPU:0, one launch (start us, length us, event | category | flops | bytes accessed | tf_op | source)
XLA Modules:
  0.0 182.1 jit_solution(2626076116855206710)
XLA Ops:
  7.2 0.0 all-reduce.4.cloned.1.call-start
  7.9 13.2 %fusion = f32[960,4096]{1,0:T(8,128)} fusion(f32[960,4096]{1,0:T(8,128)} %param.10, bf16[1,960,4096]{2,1,0:T(8,128)(2,1)} %param.9, f32[]{:T(128)S(6)} %convert_element_type.31), kind=kLoop, calls=%fused_computation.1 | loop fusion | flops 11796480 | bytes 39321604 | tf_op jit(solution)/shard_map/mul | solution.py:44
  21.1 0.0 all-reduce.4.cloned.1.call-update
  21.1 0.0 all-reduce.6.cloned.1.call-start
  21.8 11.5 %broadcast_select_fusion = (bf16[1,960,4096]{2,1,0:T(8,128)(2,1)}, bf16[1,960,4096]{2,1,0:T(8,128)(2,1)}) fusion(bf16[1,960,4096]{2,1,0:T(8,128)(2,1)} %param.13, pred[]{:T(512)S(6)} %eq.8, bf16[1,960,4096]{2,1,0:T(8,128)(2,1)} %param.12), kind=kLoop, calls=%fused_computation.15 | loop fusion | flops 7864320 | bytes 31457280 | tf_op jit(solution)/shard_map/jit(_where)/select_n | solution.py:19
  33.2 0.0 copy-start
  33.2 0.0 all-reduce.6.cloned.1.call-update
  33.3 0.8 copy-done
  34.0 0.1 copy.13
  34.1 50.4 %all_gather.3 = bf16[1,64,4096]{2,0,1:T(2,128)(2,1)S(1)} all-gather(bf16[1,4,4096]{2,0,1:T(2,128)(2,1)S(1)} %copy.13), channel_id=1, replica_groups=mesh['replica'=2,'shard'=16] {'shard'}, dimensions={1}, use_global_device_ids=true | all-gather | bytes 557056 | tf_op jit(solution)/shard_map/all_gather | solution.py:59
  84.5 0.0 copy-start.1
  84.5 0.0 all-reduce.4.cloned.1.call-done
  84.5 32.7 %multiply_subtract_fusion = (f32[960,4096]{1,0:T(8,128)}, f32[960,4096]{1,0:T(8,128)}) fusion(f32[960,4096]{1,0:T(8,128)} %param.10, f32[960,4096]{1,0:T(8,128)} %all-reduce.4.cloned.1.call-done, f32[960,4096]{1,0:T(8,128)} %param.11), kind=kLoop, calls=%fused_computation.11 | loop fusion | flops 23592960 | bytes 78643200 | tf_op jit(solution)/shard_map/sub | solution.py:48
  117.2 22.2 %all-reduce.6.cloned.1.call-done = (bf16[1,960,4096]{2,1,0:T(8,128)(2,1)}, bf16[1,960,4096]{2,1,0:T(8,128)(2,1)}) async-done(((bf16[1,960,4096]{2,1,0:T(8,128)(2,1)}, bf16[1,960,4096]{2,1,0:T(8,128)(2,1)}), (bf16[1,960,4096]{2,1,0:T(8,128)(2,1)}, bf16[1,960,4096]{2,1,0:T(8,128)(2,1)})) %all-reduce.6.cloned.1.call-update) | async-done | bytes 15728656 | tf_op jit(solution)/shard_map/psum | solution.py:20
  139.5 0.0 copy-done.1
  139.5 35.8 %fusion.6 = f32[1,960,4096]{2,1,0:T(8,128)} fusion(f32[960,4096]{1,0:T(8,128)} %get-tuple-element.5, bf16[1,960,4096]{2,1,0:T(8,128)(2,1)} %get-tuple-element.3, bf16[1,960,4096]{2,1,0:T(8,128)(2,1)} %param.13, bf16[1,960,4096]{2,1,0:T(8,128)(2,1)} %get-tuple-element.4, bf16[1,960,4096]{2,1,0:T(8,128)(2,1)} %param.12, pred[]{:T(512)S(6)} %eq.7, ...), kind=kOutput, calls=%fused_computation.8 | convolution fusion | flops 1082019840 | bytes 63561728 | tf_op jit(solution)/shard_map/dot_general | solution.py:67
Async XLA Ops:
  7.2 77.3 %all-reduce.4.cloned.1.call-start = ((), (), s32[]{:S(2)}) async-start(), calls=%async_computation | async-start | bytes 31457280 | tf_op jit(solution)/shard_map/psum | solution.py:45
  21.1 118.4 %all-reduce.6.cloned.1.call-start = ((), (), s32[]{:S(2)}) async-start(), calls=%async_computation.1 | async-start | bytes 31457280 | tf_op jit(solution)/shard_map/psum | solution.py:20
  33.2 0.8 copy-start
  84.5 55.0 %copy-start.1 = (bf16[1,960,64]{1,2,0:T(8,128)(2,1)S(1)}, bf16[1,960,64]{1,2,0:T(8,128)(2,1)}, u32[]{:S(2)}) copy-start(bf16[1,960,64]{1,2,0:T(8,128)(2,1)} %param.15) | copy-start | bytes 368644
Sparse Core Ops, SparseCore 0:
  21.2 58.5 all-reduce.3
  82.4 57.0 all-reduce.5
where the time goes:
time: 182 us
  other arithmetic  57.4 us (32%)
  blocking collectives  50.4 us (28%)
  matrix products  35.8 us (20%)
  waiting for transfers between devices  22.3 us (12%)
  between operations  15.4 us (8%)
    all_gather x1, blocking collectives, local(): tokens_part = lax.all_gather(activations, 'shard', axis=1, tiled=True)[0]  50.4 us
    dot_general x1, matrix products, local(): jnp.dot(grad_pre, tokens_part, preferred_element_type=jnp.float32) / root  35.8 us
    sub x1, other arithmetic, local(): anchor_new = anchor - outer_rate * (average + nesterov_mu * momentum_new)  32.7 us
    psum x1, waiting for transfers between devices, from_root(): return lax.psum(block, axis)  22.2 us
    mul x1, other arithmetic, local(): difference = (anchor - inner_params[0].astype(jnp.float32)) * healthy  13.2 us
    select_n x1, other arithmetic, from_root(): jnp.where(lax.axis_index(axis) == holder, block, jnp.zeros_like(block))  11.5 us
  transfers between devices with their start and end apart: 2, of which 1 were waited for; matrix products, arithmetic and copies ran while one was open for 24% of the time, Pallas kernels for 0%

commit v1 on v0

--- a/solution.py
+++ b/solution.py
@@ -1,9 +1,13 @@
+import functools
 import math
 
 import jax
 import jax.numpy as jnp
 from jax import lax
+from jax.experimental import pallas as pl
+from jax.experimental.pallas import tpu as pltpu
 from jax.sharding import PartitionSpec as P
+
 
 outer_rate = 0.7
 nesterov_mu = 0.9
@@ -14,18 +18,325 @@
 adam_eps = 1e-08
 decay_rate = 0.1
 
+UNIT = 16
+LANES = 128
+PARTS = ((4,), (6, 3, 2))
+OUTER_TILE = 64
+ADAM_TILE = 128
+DEPTH = 3
+OUTER_VMEM = 14
+ADAM_VMEM = 26
+
+
+IN_VMEM = pl.BlockSpec(memory_space=pltpu.VMEM)
+IN_HBM = pl.BlockSpec(memory_space=pl.ANY)
+IN_SMEM = pl.BlockSpec(memory_space=pltpu.SMEM)
+
+
+def in_hbm(arrays):
+    return [pltpu.with_memory_space_constraint(array, pltpu.HBM) for array in arrays]
+
+
+def in_vmem(arrays):
+    return [pltpu.with_memory_space_constraint(array, pltpu.VMEM) for array in arrays]
+
+
+def slope(pre):
+    sigma = jax.nn.sigmoid(pre)
+    return sigma * (1.0 + pre * (1.0 - sigma))
+
+
+def spans(rows, parts):
+    units, total, run, bounds = rows // UNIT, sum(parts), 0, [0]
+    for part in parts:
+        run += part
+        bounds.append(units * run // total * UNIT)
+    bounds[-1] = rows
+    return [(low, high - low) for low, high in zip(bounds, bounds[1:]) if high > low]
+
+
+def tile_of(count, limit):
+    return max(tile for tile in range(UNIT, max(limit, UNIT) + 1, UNIT) if count % tile == 0)
+
+
+def stream(steps, loads, stores, compute):
+    def load(step):
+        for source, ring, sems in loads:
+            slot = lax.rem(step, ring.shape[0])
+            pltpu.make_async_copy(source(step), ring.at[slot], sems.at[slot]).start()
+
+    def wait_load(step):
+        for source, ring, sems in loads:
+            slot = lax.rem(step, ring.shape[0])
+            pltpu.make_async_copy(source(step), ring.at[slot], sems.at[slot]).wait()
+
+    def wait_store(step):
+        for source, target, sems in stores:
+            pltpu.make_async_copy(source(step), target(step), sems.at[lax.rem(step, DEPTH)]).wait()
+
+    for step in range(min(DEPTH - 1, steps)):
+        load(step)
+
+    def body(step, carry):
+        @pl.when(step + DEPTH - 1 < steps)
+        def _():
+            load(step + DEPTH - 1)
+
+        wait_load(step)
+
+        @pl.when(step >= DEPTH)
+        def _():
+            wait_store(step - DEPTH)
+
+        compute(step, lax.rem(step, DEPTH))
+        for source, target, sems in stores:
+            pltpu.make_async_copy(source(step), target(step), sems.at[lax.rem(step, DEPTH)]).start()
+        return carry
+
+    lax.fori_loop(0, steps, body, 0)
+    for step in range(max(0, steps - DEPTH), steps):
+        wait_store(step)
+
+
+def fetch_kernel(starts, source, *rest):
+    targets, sem = rest[:-1], rest[-1]
+    copies = [
+        pltpu.make_async_copy(source.at[pl.ds(start, target.shape[0])], target, sem.at[at])
+        for at, (start, target) in enumerate(zip(starts, targets))
+    ]
+    for copy in copies:
+        copy.start()
+    for copy in copies:
+        copy.wait()
+
+
+def fetch(array, chunks):
+    width = array.shape[1]
+    return pl.pallas_call(
+        functools.partial(fetch_kernel, [start for start, _ in chunks]),
+        in_specs=[IN_HBM],
+        out_specs=[IN_VMEM] * len(chunks),
+        out_shape=[pltpu.VMEM((count, width), array.dtype) for _, count in chunks],
+        scratch_shapes=[pltpu.SemaphoreType.DMA((len(chunks),))],
+        compiler_params=pltpu.CompilerParams(vmem_limit_bytes=OUTER_VMEM * 2**20),
+        cost_estimate=pl.CostEstimate(flops=0, bytes_accessed=2 * sum(count for _, count in chunks) * width, transcendentals=0),
+        name="fetch",
+    )(*in_hbm([array]))
+
+
+def outer_kernel(start, tile, flags, own, got, anchor, momentum, *rest):
+    anchor_out, momentum_out, held, anchor_ring, momentum_ring, moved_ring, sems = rest[-7:]
+    spare = flags[0] == 1
+    rows = lambda step: pl.ds(pl.multiple_of(start + step * tile, UNIT), tile)
+
+    def compute(step, slot):
+        def with_inner(inner):
+            base = anchor_ring[slot]
+            average = base - inner[pl.ds(pl.multiple_of(step * tile, UNIT), tile), :].astype(jnp.float32)
+            moved = nesterov_mu * momentum_ring[slot] + average
+            moved_ring[slot] = moved
+            held[pl.ds(pl.multiple_of(step * tile, UNIT), tile), :] = base - outer_rate * (average + nesterov_mu * moved)
+
+        @pl.when(spare)
+        def _():
+            with_inner(got)
+
+        @pl.when(jnp.logical_not(spare))
+        def _():
+            with_inner(own)
+
+    stream(
+        own.shape[0] // tile,
+        [
+            (lambda step: anchor.at[rows(step)], anchor_ring, sems.at[0]),
+            (lambda step: momentum.at[rows(step)], momentum_ring, sems.at[1]),
+        ],
+        [
+            (lambda step: held.at[pl.ds(pl.multiple_of(step * tile, UNIT), tile)], lambda step: anchor_out.at[rows(step)], sems.at[2]),
+            (lambda step: moved_ring.at[lax.rem(step, DEPTH)], lambda step: momentum_out.at[rows(step)], sems.at[3]),
+        ],
+        compute,
+    )
+
+
+def outer_chunk(flags, own, got, anchor, momentum, start, before):
+    count, width = own.shape
+    tile = tile_of(count, OUTER_TILE)
+    whole = pltpu.HBM(anchor.shape, jnp.float32)
+    before = list(before or [])
+    ring = pltpu.VMEM((DEPTH, tile, width), jnp.float32)
+    return pl.pallas_call(
+        functools.partial(outer_kernel, start, tile),
+        in_specs=[IN_SMEM, IN_VMEM, IN_VMEM, IN_HBM, IN_HBM] + [IN_HBM, IN_HBM][: len(before)],
+        out_specs=[IN_HBM, IN_HBM, IN_VMEM],
+        out_shape=[whole, whole, pltpu.VMEM((count, width), jnp.float32)],
+        input_output_aliases={5: 0, 6: 1} if before else {},
+        scratch_shapes=[ring, ring, ring, pltpu.SemaphoreType.DMA((4, DEPTH))],
+        compiler_params=pltpu.CompilerParams(vmem_limit_bytes=OUTER_VMEM * 2**20),
+        cost_estimate=pl.CostEstimate(flops=10 * count * width, bytes_accessed=16 * count * width, transcendentals=0),
+        name="outer",
+    )(flags, *in_vmem([own, got]), *in_hbm([anchor, momentum, *before]))
+
+
+def direction(first, second, raw, root):
+    scale = math.sqrt((1.0 - beta_two) / bias_two) / root
+    scaled = raw * scale
+    mean = first * (beta_one / bias_one) + scaled * ((1.0 - beta_one) / bias_one / root / scale)
+    square = second * (beta_two / bias_two) + scaled * scaled
+    return mean * pltpu.reciprocal(square * lax.rsqrt(square) + adam_eps, approx=False)
+
+
+def adam_kernel(start, base, tile, root, pieces, flags, held, cot, first, second, got_first, got_second, *rest):
+    parts = rest[:pieces]
+    update_out, first_ring, second_ring, update_ring, tokens, sems = rest[-6:]
+    rows = lambda at, step: pl.ds(pl.multiple_of(at + step * tile, UNIT), tile)
+    height = parts[0].shape[0]
+    for index, part in enumerate(parts):
+        tokens[index * height : (index + 1) * height, :] = part[...]
+
+    def compute(step, slot):
+        weights = held[rows(start - base, step), :]
+        pre = lax.dot_general(weights.astype(jnp.bfloat16), tokens[...], (((1,), (1,)), ((), ())), preferred_element_type=jnp.float32) * (1.0 / root)
+        grad_pre = (cot[rows(start, step), : tokens.shape[0]].astype(jnp.float32) * slope(pre)).astype(jnp.bfloat16)
+        raw = jnp.dot(grad_pre, tokens[...], preferred_element_type=jnp.float32)
+        ratio = direction(first_ring[slot].astype(jnp.float32), second_ring[slot].astype(jnp.float32), raw, root)
+        update_ring[slot] = ratio + decay_rate * weights
+
+    def run(first_from, first_at, second_from, second_at):
+        stream(
+            second_count // tile,
+            [
+                (lambda step: first_from.at[rows(first_at, step)], first_ring, sems.at[0]),
+                (lambda step: second_from.at[rows(second_at, step)], second_ring, sems.at[1]),
+            ],
+            [(lambda step: update_ring.at[lax.rem(step, DEPTH)], lambda step: update_out.at[rows(start, step)], sems.at[2])],
+            compute,
+        )
+
+    second_count = got_second.shape[0]
+    takes = flags[1] == 1
+
+    @pl.when(takes)
+    def _():
+        run(got_first, start, got_second, 0)
+
+    @pl.when(jnp.logical_not(takes))
+    def _():
+        run(first, start, second, start)
+
+
+def adam_chunk(flags, held, parts, cot, first, second, got_first, got_second, start, base, before):
+    rows, width = first.shape
+    count = got_second.shape[0]
+    tile = tile_of(count, ADAM_TILE)
+    before = [] if before is None else [before]
+    ring = lambda dtype: pltpu.VMEM((DEPTH, tile, width), dtype)
+    return pl.pallas_call(
+        functools.partial(adam_kernel, start, base, tile, math.sqrt(width), len(parts)),
+        in_specs=[IN_SMEM, IN_VMEM, IN_VMEM] + [IN_HBM] * 4 + [IN_VMEM] * len(parts) + [IN_HBM] * len(before),
+        out_specs=IN_HBM,
+        out_shape=pltpu.HBM((rows, width), jnp.float32),
+        input_output_aliases={7 + len(parts): 0} if before else {},
+        scratch_shapes=[
+            ring(jnp.bfloat16),
+            ring(jnp.bfloat16),
+            ring(jnp.float32),
+            pltpu.VMEM((len(parts) * parts[0].shape[0], width), jnp.bfloat16),
+            pltpu.SemaphoreType.DMA((3, DEPTH)),
+        ],
+        compiler_params=pltpu.CompilerParams(vmem_limit_bytes=ADAM_VMEM * 2**20),
+        cost_estimate=pl.CostEstimate(flops=1000 * count * width, bytes_accessed=8 * count * width, transcendentals=2 * count * width),
+        name="adam",
+    )(flags, *in_vmem([held, cot]), *in_hbm([first, second, got_first]), got_second, *in_vmem(parts), *in_hbm(before))
+
+
+def groups_of(shards):
+    return max(size for size in range(1, shards + 1) if shards % size == 0 and size * size <= shards)
+
+
+def gather_near(block, shards):
+    group = groups_of(shards)
+    pairs = lambda shift: [(i, i // group * group + (i % group + shift) % group) for i in range(shards)]
+    return [block] + [lax.ppermute(block, "shard", pairs(shift)) for shift in range(1, group)]
+
+
+def gather_far(block, shards):
+    group = groups_of(shards)
+    count = shards // group
+    pairs = lambda shift: [(i, (i // group + shift) % count * group + i % group) for i in range(shards)]
+    return [block] + [lax.ppermute(block, "shard", pairs(shift)) for shift in range(1, count)]
+
+
+def sources(shards):
+    group = groups_of(shards)
+    count = shards // group
+    me, slot = lax.axis_index("shard"), jnp.arange(shards, dtype=jnp.int32)
+    return (me // group + count - slot // group) % count * group + (me % group + group - slot % group) % group
+
+
+def pair_step(inner_params, anchor, momentum, first_moment, second_moment, activations, cotangent, spare_index, peer_index):
+    position = lax.axis_index("replica")
+    shards = lax.axis_size("shard")
+    rows = anchor.shape[0]
+
+    def swap(array):
+        return lax.ppermute(array, "replica", [(0, 1), (1, 0)])
+
+    spare, peer = spare_index[0], peer_index[0]
+    flags = jnp.stack([position == spare, (position == spare) & (peer != position)]).astype(jnp.int32)
+    inner, first, second = inner_params[0], first_moment[0], second_moment[0]
+
+    here, cot = activations[0], cotangent[0]
+    depth = here.shape[0]
+    column = jnp.arange(shards * depth, dtype=jnp.int32)
+    token_of = jnp.repeat(sources(shards), depth) * depth + column % depth
+    token_of = jnp.pad(token_of, (0, -len(column) % LANES), constant_values=-1)
+    inner, flags, token_of = lax.optimization_barrier((inner, flags, token_of))
+
+    chunks = spans(rows, [sum(group) for group in PARTS])
+    pieces = [
+        (start + low, high, start, which)
+        for which, ((start, count), group) in enumerate(zip(chunks, PARTS))
+        for low, high in spans(count, group)
+    ]
+    own_inner, got_inner = [], []
+    for chunk in chunks:
+        if own_inner:
+            inner, own_inner[-1] = lax.optimization_barrier((inner, own_inner[-1]))
+        own_inner += fetch(inner, [chunk])
+        got_inner.append(swap(own_inner[-1]))
+    first, own_inner[-1] = lax.optimization_barrier((first, own_inner[-1]))
+    got_first = swap(first)
+
+    near = gather_near(here, shards)
+    token = jnp.arange(cot.shape[1], dtype=jnp.int32)[:, None]
+    place = (token == token_of[None, :]).astype(jnp.bfloat16)
+    cot = jnp.dot(cot, place, preferred_element_type=jnp.float32).astype(jnp.bfloat16)
+
+    state, helds, parts, got_second = None, [], None, []
+    for (start, count), own, got in zip(chunks, own_inner, got_inner):
+        *state, held = outer_chunk(flags, own, got, anchor, momentum, start, state)
+        helds.append(held)
+        if parts is None:
+            near, second, state = lax.optimization_barrier((near, second, state))
+            parts = gather_far(jnp.concatenate(near, 0), shards)
+            for block in fetch(second, [piece[:2] for piece in pieces]):
+                got_second.append(swap(block))
+    parts, state = lax.optimization_barrier((parts, state))
+    anchor_new, momentum_new = state
+
+    update = None
+    for (start, count, base, which), got in zip(pieces, got_second):
+        update = adam_chunk(flags, helds[which], parts, cot, first, second, got_first, got, start, base, update)
+    return anchor_new, momentum_new, update[None]
+
 
 def from_root(block, axis, holder):
     block = jnp.where(lax.axis_index(axis) == holder, block, jnp.zeros_like(block))
     return lax.psum(block, axis)
 
 
-def slope(pre):
-    sigma = jax.nn.sigmoid(pre)
-    return sigma * (1.0 + pre * (1.0 - sigma))
-
-
-def local(
+def general_step(
     inner_params,
     anchor,
     momentum,
@@ -83,6 +394,7 @@
         P("shard"),
         P("shard"),
     )
+    local = pair_step if mesh.shape["replica"] == 2 else general_step
     return jax.shard_map(
         local,
         mesh=mesh,

time: 182 us -> 114 us (0.63)
  Pallas kernels: 0 us -> 61.3 us
  other arithmetic: 57.4 us -> 0.18 us
  blocking collectives: 50.4 us -> 0 us
  matrix products: 35.8 us -> 0.29 us
  starting transfers between devices: 0.08 us -> 14.9 us
  between operations: 15.4 us -> 2.32 us
  waiting for transfers between devices: 22.3 us -> 34.1 us
    pallas_call x0 -> x9, Pallas kernels: none -> 61.3 us  [the longest x4 27.3 us: adam_chunk(): pl.pallas_call(functools.partial(adam_kernel, start, base, tile, math.sqr...]
    all_gather x1 -> x0, blocking collectives: 50.4 us -> none  [local(): tokens_part = lax.all_gather(activations, 'shard', axis=1, tiled=True)[0]]
    dot_general x1, matrix products: 35.8 us -> 0.29 us  [pair_step(): jnp.dot(cot, place, preferred_element_type=jnp.float32).astype(jnp.bfloat16)]
    ppermute x0 -> x13, waiting for transfers between devices: none -> 34.1 us  [the longest x7 18.9 us: swap(): return lax.ppermute(array, 'replica', [(0, 1), (1, 0)])]
    sub x1 -> x0, other arithmetic: 32.7 us -> none  [local(): anchor_new = anchor - outer_rate * (average + nesterov_mu * momentum_new)]
    psum x2 -> x0, waiting for transfers between devices: 22.2 us -> none  [the longest x1 22.2 us: from_root(): return lax.psum(block, axis)]
    ppermute x0 -> x13, starting transfers between devices: none -> 14.9 us  [the longest x3 7.88 us: gather_near(): lax.ppermute(block, 'shard', pairs(shift))]
    mul x1, other arithmetic: 13.2 us -> 0.01 us  [pair_step(): token_of = jnp.repeat(sources(shards), depth) * depth + column % depth]
  transfers between devices with their start and end apart: 2 -> 13, of which waited for: 1 -> 4; matrix products, arithmetic and copies ran while one was open for 24% -> 0% of each run, Pallas kernels for 0% -> 46%
where the time goes in v1:
time: 114 us; the launch traced here: 113 us
  Pallas kernels  61.3 us (54%)
  waiting for transfers between devices  34.1 us (30%)
  starting transfers between devices  14.9 us (13%)
  between operations  2.32 us (2%)
    pallas_call x4, Pallas kernels, adam_chunk(): pl.pallas_call(functools.partial(adam_kernel, start, base, tile, math.sqr...  27.3 us
    pallas_call x2, Pallas kernels, outer_chunk(): pl.pallas_call(functools.partial(outer_kernel, start, tile), in_specs=[IN...  24.7 us
    ppermute x7, waiting for transfers between devices, swap(): return lax.ppermute(array, 'replica', [(0, 1), (1, 0)])  18.9 us
    ppermute x3, waiting for transfers between devices, gather_far(): lax.ppermute(block, 'shard', pairs(shift))  15.2 us
    pallas_call x3, Pallas kernels, fetch(): pl.pallas_call(functools.partial(fetch_kernel, [start for start, _ in chu...  9.29 us
    ppermute x3, starting transfers between devices, gather_near(): lax.ppermute(block, 'shard', pairs(shift))  7.88 us
    ppermute x3, starting transfers between devices, gather_far(): lax.ppermute(block, 'shard', pairs(shift))  4.83 us
  transfers between devices with their start and end apart: 13, of which 4 were waited for; matrix products, arithmetic and copies ran while one was open for 0% of the time, Pallas kernels for 46%

profile of v1, /device:TPU:0, one launch (start us, length us, event | category | flops | bytes accessed | tf_op | source)
XLA Modules:
  0.0 113.2 jit_solution(1588927209897442699)
XLA Ops:
  0.6 0.0 copy-start
  0.7 0.1 broadcast_in_dim.8
  0.8 0.1 mul.15
  2.2 0.1 add_convert_fusion.flags
  2.3 1.6 %fetch.3.own = bf16[256,4096]{1,0:T(8,128)(2,1)S(1)} custom-call(bf16[960,4096]{1,0:T(8,128)(2,1)} %bitcast.22), custom_call_target="tpu_custom_call" | custom-call | bytes 2097152 | tf_op jit(solution)/shard_map/fetch/pallas_call | solution.py:115
  3.9 0.0 copy-start.2
  3.9 2.6 %fetch.4.own = bf16[704,4096]{1,0:T(8,128)(2,1)S(1)} custom-call(bf16[960,4096]{1,0:T(8,128)(2,1)} %bitcast.23), custom_call_target="tpu_custom_call" | custom-call | bytes 5767168 | tf_op jit(solution)/shard_map/fetch/pallas_call | solution.py:115
  6.5 0.6 collective-permute-start.8
  7.1 0.1 collective-permute-start.7
  7.2 0.4 collective-permute-start.3
  7.6 0.0 copy-done.2
  7.6 2.6 %collective-permute-start = (bf16[4,4096]{1,0:T(4,128)(2,1)S(1)}, bf16[4,4096]{1,0:T(4,128)(2,1)S(1)}, u32[]{:S(2)}, u32[]{:S(2)}) collective-permute-start(bf16[4,4096]{1,0:T(4,128)(2,1)S(1)} %bitcast.24), channel_id=1, source_target_pairs={{0,1},{1,2},{2,3},{3,0},{4,5},{5,6},{6,7},{7,4},{8,9},{9,10},{10,1... | collective-permute-start | bytes 98312 | tf_op jit(solution)/shard_map/ppermute | solution.py:260
  10.2 1.5 %collective-permute-start.1 = (bf16[4,4096]{1,0:T(4,128)(2,1)S(1)}, bf16[4,4096]{1,0:T(4,128)(2,1)S(1)}, u32[]{:S(2)}, u32[]{:S(2)}) collective-permute-start(bf16[4,4096]{1,0:T(4,128)(2,1)S(1)} %bitcast.25), channel_id=1, source_target_pairs={{0,2},{1,3},{2,0},{3,1},{4,6},{5,7},{6,4},{7,5},{8,10},{9,11},{10,... | collective-permute-start | bytes 98312 | tf_op jit(solution)/shard_map/ppermute | solution.py:260
  11.7 18.9 %collective-permute-done.3.got = bf16[256,4096]{1,0:T(8,128)(2,1)S(1)} collective-permute-done((bf16[256,4096]{1,0:T(8,128)(2,1)S(1)}, bf16[256,4096]{1,0:T(8,128)(2,1)S(1)}, u32[]{:S(2)}, u32[]{:S(2)}) %collective-permute-start.3) | collective-permute-done | bytes 2097184 | tf_op jit(solution)/shard_map/ppermute | solution.py:283
  30.6 3.8 %collective-permute-start.2 = (bf16[4,4096]{1,0:T(4,128)(2,1)S(1)}, bf16[4,4096]{1,0:T(4,128)(2,1)S(1)}, u32[]{:S(2)}, u32[]{:S(2)}) collective-permute-start(bf16[4,4096]{1,0:T(4,128)(2,1)S(1)} %bitcast.26), channel_id=1, source_target_pairs={{0,3},{1,0},{2,1},{3,2},{4,7},{5,4},{6,5},{7,6},{8,11},{9,8},{10,9... | collective-permute-start | bytes 98312 | tf_op jit(solution)/shard_map/ppermute | solution.py:260
  34.4 7.6 %outer.2 = (f32[960,4096]{1,0:T(8,128)}, f32[960,4096]{1,0:T(8,128)}, f32[256,4096]{1,0:T(8,128)S(1)}) custom-call(s32[2]{0:T(128)S(1)} %add_convert_fusion.flags, bf16[256,4096]{1,0:T(8,128)(2,1)S(1)} %fetch.3.own, bf16[256,4096]{1,0:T(8,128)(2,1)S(1)} %collective-permute-done.3.got, f32[960,4096]{1,0:T(8,128)} %anchor.3, f32[960,4096]{1,0:T(8,128)} %momentum.3), custom_call_target="tpu_custom_call" | custom-call | flops 10485760 | bytes 16777216 | tf_op jit(solution)/shard_map/outer/pallas_call | solution.py:168
  42.0 0.0 collective-permute-done
  42.0 0.0 collective-permute-done.1
  42.0 0.0 collective-permute-done.2
  42.0 5.0 %fetch.5 = (bf16[256,4096]{1,0:T(8,128)(2,1)S(1)}, bf16[384,4096]{1,0:T(8,128)(2,1)}, bf16[192,4096]{1,0:T(8,128)(2,1)S(1)}, bf16[128,4096]{1,0:T(8,128)(2,1)S(1)}) custom-call(bf16[960,4096]{1,0:T(8,128)(2,1)} %bitcast.17), custom_call_target="tpu_custom_call" | custom-call | bytes 7864320 | tf_op jit(solution)/shard_map/fetch/pallas_call | solution.py:115
  47.1 0.1 collective-permute-start.11
  47.1 0.5 collective-permute-start.12
  47.6 0.1 pad_maximum_fusion.rest_0_
  47.7 1.6 %collective-permute-start.4 = (bf16[16,4096]{1,0:T(8,128)(2,1)S(1)}, bf16[16,4096]{1,0:T(8,128)(2,1)S(1)}, u32[]{:S(2)}, u32[]{:S(2)}) collective-permute-start(bf16[16,4096]{1,0:T(8,128)(2,1)S(1)} %pad_maximum_fusion.rest_0_), channel_id=1, source_target_pairs={{0,4},{1,5},{2,6},{3,7},{4,8},{5,9},{6,10},{7,11},{8,12},{9,13},{1... | collective-permute-start | bytes 393224 | tf_op jit(solution)/shard_map/ppermute | solution.py:267
  49.4 5.8 %collective-permute-done.4.rest_1_ = bf16[16,4096]{1,0:T(8,128)(2,1)S(1)} collective-permute-done((bf16[16,4096]{1,0:T(8,128)(2,1)S(1)}, bf16[16,4096]{1,0:T(8,128)(2,1)S(1)}, u32[]{:S(2)}, u32[]{:S(2)}) %collective-permute-start.4) | collective-permute-done | bytes 131104 | tf_op jit(solution)/shard_map/ppermute | solution.py:267
  55.1 0.7 collective-permute-start.5
  55.9 6.8 %collective-permute-done.5.rest_2_ = bf16[16,4096]{1,0:T(8,128)(2,1)S(1)} collective-permute-done((bf16[16,4096]{1,0:T(8,128)(2,1)S(1)}, bf16[16,4096]{1,0:T(8,128)(2,1)S(1)}, u32[]{:S(2)}, u32[]{:S(2)}) %collective-permute-start.5) | collective-permute-done | bytes 131104 | tf_op jit(solution)/shard_map/ppermute | solution.py:267
  62.6 2.5 %collective-permute-start.6 = (bf16[16,4096]{1,0:T(8,128)(2,1)S(1)}, bf16[16,4096]{1,0:T(8,128)(2,1)S(1)}, u32[]{:S(2)}, u32[]{:S(2)}) collective-permute-start(bf16[16,4096]{1,0:T(8,128)(2,1)S(1)} %pad_maximum_fusion.rest_0_), channel_id=1, source_target_pairs={{0,12},{1,13},{2,14},{3,15},{4,0},{5,1},{6,2},{7,3},{8,4},{9,5},{1... | collective-permute-start | bytes 393224 | tf_op jit(solution)/shard_map/ppermute | solution.py:267
  65.1 2.7 %collective-permute-done.6.rest_3_ = bf16[16,4096]{1,0:T(8,128)(2,1)S(1)} collective-permute-done((bf16[16,4096]{1,0:T(8,128)(2,1)S(1)}, bf16[16,4096]{1,0:T(8,128)(2,1)S(1)}, u32[]{:S(2)}, u32[]{:S(2)}) %collective-permute-start.6) | collective-permute-done | bytes 131104 | tf_op jit(solution)/shard_map/ppermute | solution.py:267
  67.8 0.0 collective-permute-start.10
  67.8 0.0 collective-permute-done.7.got
  67.8 0.5 collective-permute-start.9
  68.3 0.0 copy-done
  68.3 0.3 fusion.cot
  68.6 17.1 %outer.3 = (f32[960,4096]{1,0:T(8,128)}, f32[960,4096]{1,0:T(8,128)}, f32[704,4096]{1,0:T(8,128)S(1)}) custom-call(s32[2]{0:T(128)S(1)} %add_convert_fusion.flags, bf16[704,4096]{1,0:T(8,128)(2,1)S(1)} %fetch.4.own, bf16[704,4096]{1,0:T(8,128)(2,1)S(1)} %collective-permute-done.7.got, ...), custom_call_target="tpu_custom_call", output_to_operand_aliasing={{0}: (5, {}), {1}: (6, {})} | custom-call | flops 28835840 | bytes 46137344 | tf_op jit(solution)/shard_map/outer/pallas_call | solution.py:168
  85.7 0.0 collective-permute-done.12.got_second
  85.7 0.0 collective-permute-done.8.got_first
  85.7 7.1 %adam.4.rest_4_ = f32[960,4096]{1,0:T(8,128)} custom-call(s32[2]{0:T(128)S(1)} %add_convert_fusion.flags, f32[256,4096]{1,0:T(8,128)S(1)} %get-tuple-element.61.held, bf16[960,128]{1,0:T(8,128)(2,1)S(1)} %fusion.cot, bf16[960,4096]{1,0:T(8,128)(2,1)} %bitcast.7.first, bf16[960,4096]{1,0:T(8,128)(2,1)} %bitcast.18, ...), custom_call_target="tpu_custom_call" | custom-call | flops 1048576000 | bytes 8388608 | tf_op jit(solution)/shard_map/adam/pallas_call | solution.py:234
  92.8 0.0 collective-permute-done.11.got_second
  92.8 9.1 %adam.5.rest_4_ = f32[960,4096]{1,0:T(8,128)} custom-call(s32[2]{0:T(128)S(1)} %add_convert_fusion.flags, f32[704,4096]{1,0:T(8,128)S(1)} %get-tuple-element.50.held, bf16[960,128]{1,0:T(8,128)(2,1)S(1)} %fusion.cot, bf16[960,4096]{1,0:T(8,128)(2,1)} %bitcast.7.first, bf16[960,4096]{1,0:T(8,128)(2,1)} %bitcast.19, ...), custom_call_target="tpu_custom_call", output_to_operand_aliasing={{}: (11, {})} | custom-call | flops 1572864000 | bytes 12582912 | tf_op jit(solution)/shard_map/adam/pallas_call | solution.py:234
  101.9 0.0 collective-permute-done.10.got_second
  101.9 6.0 %adam.6.rest_4_ = f32[960,4096]{1,0:T(8,128)} custom-call(s32[2]{0:T(128)S(1)} %add_convert_fusion.flags, f32[704,4096]{1,0:T(8,128)S(1)} %get-tuple-element.50.held, bf16[960,128]{1,0:T(8,128)(2,1)S(1)} %fusion.cot, bf16[960,4096]{1,0:T(8,128)(2,1)} %bitcast.7.first, bf16[960,4096]{1,0:T(8,128)(2,1)} %bitcast.20, ...), custom_call_target="tpu_custom_call", output_to_operand_aliasing={{}: (11, {})} | custom-call | flops 786432000 | bytes 6291456 | tf_op jit(solution)/shard_map/adam/pallas_call | solution.py:234
  107.9 0.0 collective-permute-done.9.got_second
  107.9 0.0 copy-start.1
  107.9 5.2 %adam.7 = f32[960,4096]{1,0:T(8,128)} custom-call(s32[2]{0:T(128)S(1)} %add_convert_fusion.flags, f32[704,4096]{1,0:T(8,128)S(1)} %get-tuple-element.50.held, bf16[960,128]{1,0:T(8,128)(2,1)S(1)} %fusion.cot, bf16[960,4096]{1,0:T(8,128)(2,1)} %bitcast.7.first, bf16[960,4096]{1,0:T(8,128)(2,1)} %bitcast.21, ...), custom_call_target="tpu_custom_call", output_to_operand_aliasing={{}: (11, {})} | custom-call | flops 524288000 | bytes 4194304 | tf_op jit(solution)/shard_map/adam/pallas_call | solution.py:234
  113.1 0.0 copy-done.1
  (3 shorter events, 0.0 us)
Async XLA Ops:
  0.6 67.7 %copy-start = (bf16[1,960,64]{1,2,0:T(8,128)(2,1)S(1)}, bf16[1,960,64]{1,2,0:T(8,128)(2,1)}, u32[]{:S(2)}) copy-start(bf16[1,960,64]{1,2,0:T(8,128)(2,1)} %param.15) | copy-start | bytes 368644
  3.9 3.7 %copy-start.2 = (bf16[1,4,4096]{2,1,0:T(4,128)(2,1)S(1)}, bf16[1,4,4096]{2,1,0:T(4,128)(2,1)}, u32[]{:S(2)}) copy-start(bf16[1,4,4096]{2,1,0:T(4,128)(2,1)} %param.14) | copy-start | bytes 98308
  6.5 79.2 %collective-permute-start.8 = (bf16[960,4096]{1,0:T(8,128)(2,1)}, bf16[960,4096]{1,0:T(8,128)(2,1)}, u32[]{:S(2)}, u32[]{:S(2)}) collective-permute-start(bf16[960,4096]{1,0:T(8,128)(2,1)} %bitcast.7.first), channel_id=1, source_target_pairs={{0,16},{16,0},{1,17},{17,1},{2,18},{18,2},{3,19},{19,3},{4,20},{20... | collective-permute-start | bytes 23592968 | tf_op jit(solution)/shard_map/ppermute | solution.py:283
  7.1 60.7 %collective-permute-start.7 = (bf16[704,4096]{1,0:T(8,128)(2,1)S(1)}, bf16[704,4096]{1,0:T(8,128)(2,1)S(1)}, u32[]{:S(2)}, u32[]{:S(2)}) collective-permute-start(bf16[704,4096]{1,0:T(8,128)(2,1)S(1)} %fetch.4.own), channel_id=1, source_target_pairs={{0,16},{16,0},{1,17},{17,1},{2,18},{18,2},{3,19},{19,3},{4,20},{20... | collective-permute-start | bytes 17301512 | tf_op jit(solution)/shard_map/ppermute | solution.py:283
  7.2 23.4 %collective-permute-start.3 = (bf16[256,4096]{1,0:T(8,128)(2,1)S(1)}, bf16[256,4096]{1,0:T(8,128)(2,1)S(1)}, u32[]{:S(2)}, u32[]{:S(2)}) collective-permute-start(bf16[256,4096]{1,0:T(8,128)(2,1)S(1)} %fetch.3.own), channel_id=1, source_target_pairs={{0,16},{16,0},{1,17},{17,1},{2,18},{18,2},{3,19},{19,3},{4,20},{20... | collective-permute-start | bytes 6291464 | tf_op jit(solution)/shard_map/ppermute | solution.py:283
  7.6 34.4 %collective-permute-start = (bf16[4,4096]{1,0:T(4,128)(2,1)S(1)}, bf16[4,4096]{1,0:T(4,128)(2,1)S(1)}, u32[]{:S(2)}, u32[]{:S(2)}) collective-permute-start(bf16[4,4096]{1,0:T(4,128)(2,1)S(1)} %bitcast.24), channel_id=1, source_target_pairs={{0,1},{1,2},{2,3},{3,0},{4,5},{5,6},{6,7},{7,4},{8,9},{9,10},{10,1... | collective-permute-start | bytes 98312 | tf_op jit(solution)/shard_map/ppermute | solution.py:260
  10.2 31.8 %collective-permute-start.1 = (bf16[4,4096]{1,0:T(4,128)(2,1)S(1)}, bf16[4,4096]{1,0:T(4,128)(2,1)S(1)}, u32[]{:S(2)}, u32[]{:S(2)}) collective-permute-start(bf16[4,4096]{1,0:T(4,128)(2,1)S(1)} %bitcast.25), channel_id=1, source_target_pairs={{0,2},{1,3},{2,0},{3,1},{4,6},{5,7},{6,4},{7,5},{8,10},{9,11},{10,... | collective-permute-start | bytes 98312 | tf_op jit(solution)/shard_map/ppermute | solution.py:260
  30.6 11.4 %collective-permute-start.2 = (bf16[4,4096]{1,0:T(4,128)(2,1)S(1)}, bf16[4,4096]{1,0:T(4,128)(2,1)S(1)}, u32[]{:S(2)}, u32[]{:S(2)}) collective-permute-start(bf16[4,4096]{1,0:T(4,128)(2,1)S(1)} %bitcast.26), channel_id=1, source_target_pairs={{0,3},{1,0},{2,1},{3,2},{4,7},{5,4},{6,5},{7,6},{8,11},{9,8},{10,9... | collective-permute-start | bytes 98312 | tf_op jit(solution)/shard_map/ppermute | solution.py:260
  47.1 45.7 %collective-permute-start.11 = (bf16[384,4096]{1,0:T(8,128)(2,1)}, bf16[384,4096]{1,0:T(8,128)(2,1)S(1)}, u32[]{:S(2)}, u32[]{:S(2)}) collective-permute-start(bf16[384,4096]{1,0:T(8,128)(2,1)} %get-tuple-element.60), channel_id=1, source_target_pairs={{0,16},{16,0},{1,17},{17,1},{2,18},{18,2},{3,19},{19,3},{4,20},{20... | collective-permute-start | bytes 9437192 | tf_op jit(solution)/shard_map/ppermute | solution.py:283
  47.1 38.5 %collective-permute-start.12 = (bf16[256,4096]{1,0:T(8,128)(2,1)S(1)}, bf16[256,4096]{1,0:T(8,128)(2,1)S(1)}, u32[]{:S(2)}, u32[]{:S(2)}) collective-permute-start(bf16[256,4096]{1,0:T(8,128)(2,1)S(1)} %get-tuple-element.62), channel_id=1, source_target_pairs={{0,16},{16,0},{1,17},{17,1},{2,18},{18,2},{3,19},{19,3},{4,20},{20... | collective-permute-start | bytes 6291464 | tf_op jit(solution)/shard_map/ppermute | solution.py:283
  47.7 7.4 %collective-permute-start.4 = (bf16[16,4096]{1,0:T(8,128)(2,1)S(1)}, bf16[16,4096]{1,0:T(8,128)(2,1)S(1)}, u32[]{:S(2)}, u32[]{:S(2)}) collective-permute-start(bf16[16,4096]{1,0:T(8,128)(2,1)S(1)} %pad_maximum_fusion.rest_0_), channel_id=1, source_target_pairs={{0,4},{1,5},{2,6},{3,7},{4,8},{5,9},{6,10},{7,11},{8,12},{9,13},{1... | collective-permute-start | bytes 393224 | tf_op jit(solution)/shard_map/ppermute | solution.py:267
  55.1 7.5 %collective-permute-start.5 = (bf16[16,4096]{1,0:T(8,128)(2,1)S(1)}, bf16[16,4096]{1,0:T(8,128)(2,1)S(1)}, u32[]{:S(2)}, u32[]{:S(2)}) collective-permute-start(bf16[16,4096]{1,0:T(8,128)(2,1)S(1)} %pad_maximum_fusion.rest_0_), channel_id=1, source_target_pairs={{0,8},{1,9},{2,10},{3,11},{4,12},{5,13},{6,14},{7,15},{8,0},{9,1},... | collective-permute-start | bytes 393224 | tf_op jit(solution)/shard_map/ppermute | solution.py:267
  62.6 5.2 %collective-permute-start.6 = (bf16[16,4096]{1,0:T(8,128)(2,1)S(1)}, bf16[16,4096]{1,0:T(8,128)(2,1)S(1)}, u32[]{:S(2)}, u32[]{:S(2)}) collective-permute-start(bf16[16,4096]{1,0:T(8,128)(2,1)S(1)} %pad_maximum_fusion.rest_0_), channel_id=1, source_target_pairs={{0,12},{1,13},{2,14},{3,15},{4,0},{5,1},{6,2},{7,3},{8,4},{9,5},{1... | collective-permute-start | bytes 393224 | tf_op jit(solution)/shard_map/ppermute | solution.py:267
  67.8 34.1 %collective-permute-start.10 = (bf16[192,4096]{1,0:T(8,128)(2,1)S(1)}, bf16[192,4096]{1,0:T(8,128)(2,1)S(1)}, u32[]{:S(2)}, u32[]{:S(2)}) collective-permute-start(bf16[192,4096]{1,0:T(8,128)(2,1)S(1)} %get-tuple-element.59), channel_id=1, source_target_pairs={{0,16},{16,0},{1,17},{17,1},{2,18},{18,2},{3,19},{19,3},{4,20},{20... | collective-permute-start | bytes 4718600 | tf_op jit(solution)/shard_map/ppermute | solution.py:283
  67.8 40.1 %collective-permute-start.9 = (bf16[128,4096]{1,0:T(8,128)(2,1)S(1)}, bf16[128,4096]{1,0:T(8,128)(2,1)S(1)}, u32[]{:S(2)}, u32[]{:S(2)}) collective-permute-start(bf16[128,4096]{1,0:T(8,128)(2,1)S(1)} %get-tuple-element.54), channel_id=1, source_target_pairs={{0,16},{16,0},{1,17},{17,1},{2,18},{18,2},{3,19},{19,3},{4,20},{20... | collective-permute-start | bytes 3145736 | tf_op jit(solution)/shard_map/ppermute | solution.py:283
  107.9 5.2 %copy-start.1 = (bf16[1,960,64]{1,2,0:T(8,128)(2,1)S(1)}, bf16[1,960,64]{1,2,0:T(8,128)(2,1)}, u32[]{:S(2)}) copy-start(bf16[1,960,64]{1,2,0:T(8,128)(2,1)} %param.15) | copy-start | bytes 368644
